TPU v7x, 1024 devices: a whole 4x8x16 slice. The times are simulated.
1024 devices in a mesh: qa: 32 (over z_lo, x), qb: 32 (over z_hi, y, core).
Axes of the slice: x: 4, y: 8, z: 16 (z_hi: 2, z_lo: 8; z = z_hi * 8 + z_lo), core: 2. Of those that a mesh axis runs over, the one named last changes fastest.
Arguments:
- amplitudes: bfloat16 [2, 32, 32, 4, 128, 128], P(None, 'qa', 'qb'), may hold values from -6 to 6
- layer_gates: bfloat16 [8, 2, 128, 128], replicated, may hold values from -0.375 to 0.375
- pauli_blocks: bfloat16 [4, 2, 128, 128], replicated, may hold values from -0.375 to 0.375
- flip_masks: int32 [4], replicated, may hold values from 0 to 127
- phase_masks: int32 [4], replicated, may hold values from 0 to 131071
Outputs:
- final_state: bfloat16 [2, 32, 32, 4, 128, 128], P(None, 'qa', 'qb')
- pauli_image: float32 [2, 32, 32, 4, 128, 128], P(None, 'qa', 'qb')
All inputs are finite; a program needn't handle non-finite values.
Results may differ from a plain program's by a relative error of at most 0.014.
Values may be sent and summed in bfloat16 or wider, within the bound.
No kernel may reach another device: no remote copies, remote signals or barrier semaphores. Data moves between devices by JAX's collectives and lax.ppermute only.
A program may use at most 32 MiB of HBM per device.

v0:
```python
import jax
import jax.numpy as jnp
import numpy as np
from jax import lax
from jax.experimental import pallas as pl
from jax.experimental.pallas import tpu as pltpu
from jax.sharding import Mesh, PartitionSpec as P

FINE = ("zl2", "zl", "x1", "x0", "zh", "y", "c")
FINE_SIZES = (2, 4, 2, 2, 2, 8, 2)
E1 = ("zh", "zl2", "zl", "x1", "x0")
E2 = ("zl", "x1", "x0", "y", "c")
E3 = ("zh", "zl2", "x0", "y", "c")
BF = jnp.bfloat16
F32 = jnp.float32
NT = (((1,), (1,)), ((), ()))
NN = (((1,), (0,)), ((), ()))


def exchange(value, axes):
    return lax.all_to_all(value, axes, split_axis=0, concat_axis=0, tiled=True)


def parity_sign(value):
    for shift in (16, 8, 4, 2, 1):
        value = jnp.bitwise_xor(value, jnp.right_shift(value, shift))
    return (1 - 2 * jnp.bitwise_and(value, 1)).astype(F32)


def reorder(sizes, perm):
    source = np.arange(int(np.prod(sizes))).reshape(sizes).transpose(perm).reshape(-1)
    return (source[:, None] == np.arange(source.size)[None, :]).astype(np.float32)


def dot(a, b, dims):
    return lax.dot_general(a, b, dims, preferred_element_type=F32)


def swap_pair(x0, x1, shift, lane):
    low = jnp.bitwise_and(lane, shift) == 0
    return (
        jnp.where(low, x0, pltpu.roll(x1, shift, 1)),
        jnp.where(low, pltpu.roll(x0, 128 - shift, 1), x1),
    )


def swap_quads(t, hi, lo, lane):
    a0, a2 = swap_pair(t[0], t[2], hi, lane)
    a1, a3 = swap_pair(t[1], t[3], hi, lane)
    b0, b1 = swap_pair(a0, a1, lo, lane)
    b2, b3 = swap_pair(a2, a3, lo, lane)
    return b0, b1, b2, b3


def lanes_of(rows):
    return lax.broadcasted_iota(jnp.int32, (rows, 128), 1)


def regroup(d_ref, q_ref, hi, lo):
    lane = lanes_of(32)
    for p in range(2):
        for g in range(4):
            t = [d_ref[pl.ds(p * 128 + i * 32, 32), pl.ds(g * 128, 128)] for i in range(4)]
            for s, block in enumerate(swap_quads(t, hi, lo, lane)):
                q_ref[pl.ds(g * 128 + s * 32, 32), pl.ds(p * 128, 128)] = block.astype(BF)


def pre_kernel(amp_ref, pr_ref, pc_ref, pm_ref, out_ref, z_ref):
    lane = lanes_of(32)
    for e in range(4):
        for p in range(2):
            turned = dot(pr_ref[...], amp_ref[p, e], NN).astype(BF)
            y = dot(pc_ref[...], turned, NT)
            t = [y[i * 32 : (i + 1) * 32] for i in range(4)]
            for i, block in enumerate(swap_quads(t, 64, 32, lane)):
                z_ref[pl.ds(p * 128 + i * 32, 32), pl.ds(e * 128, 128)] = block.astype(BF)
    moved = dot(pm_ref[...], z_ref[...], NN).astype(BF)
    for e in range(4):
        out_ref[pl.ds(e * 256, 256), :] = moved[:, e * 128 : (e + 1) * 128]


PR = reorder((32, 4), (1, 0))
PC = reorder((16, 2, 4), (2, 0, 1))
PM1 = reorder((2, 4, 16, 2), (2, 3, 0, 1))


def pre(amplitudes):
    out = pl.pallas_call(
        pre_kernel,
        out_shape=jax.ShapeDtypeStruct((1024, 128), BF),
        scratch_shapes=[pltpu.VMEM((256, 512), BF)],
        name="pre",
    )(amplitudes.reshape(2, 4, 128, 128), jnp.asarray(PR, BF), jnp.asarray(PC, BF), jnp.asarray(PM1, BF))
    return out.reshape(64, 16, 128)


def row_kernel(r_ref, v_ref, out_ref, x_ref, d_ref, q_ref):
    for b4 in range(2):
        x = r_ref[pl.ds(b4 * 512, 512), :].astype(F32).reshape(32, 2, 8, 128)
        for c1 in range(2):
            x_ref[:, pl.ds((b4 * 2 + c1) * 128, 128)] = x[:, c1].reshape(256, 128).astype(BF)
    d_ref[...] = dot(v_ref[0], x_ref[...], NN)
    regroup(d_ref, q_ref, 64, 32)
    d_ref[...] = dot(v_ref[1], q_ref[...], NT)
    regroup(d_ref, q_ref, 64, 32)
    d_ref[...] = dot(v_ref[2], q_ref[...], NT)
    regroup(d_ref, q_ref, 64, 32)
    d_ref[...] = dot(v_ref[3], q_ref[...], NT)
    lane = lanes_of(32)
    for piece in range(4):
        x = {}
        for p in range(2):
            for g in range(4):
                x[g >> 1, g & 1, p] = d_ref[pl.ds(p * 128 + piece * 32, 32), pl.ds(g * 128, 128)]
        for c1 in range(2):
            for p in range(2):
                x[0, c1, p], x[1, c1, p] = swap_pair(x[0, c1, p], x[1, c1, p], 8, lane)
        for b in range(2):
            for p in range(2):
                x[b, 0, p], x[b, 1, p] = swap_pair(x[b, 0, p], x[b, 1, p], 4, lane)
        for b in range(2):
            for c1 in range(2):
                x[b, c1, 0], x[b, c1, 1] = swap_pair(x[b, c1, 0], x[b, c1, 1], 2, lane)
        for (i, j, k), block in x.items():
            out_ref[pl.ds((i * 4 + j * 2 + k) * 128 + piece * 32, 32), :] = block.astype(BF)


def row_phase(r1, row):
    out = pl.pallas_call(
        row_kernel,
        out_shape=jax.ShapeDtypeStruct((1024, 128), BF),
        scratch_shapes=[pltpu.VMEM((256, 512), BF), pltpu.VMEM((256, 512), F32), pltpu.VMEM((512, 256), BF)],
        name="rows",
    )(r1.reshape(1024, 128), row)
    return out.reshape(256, 4, 128)


def col_kernel(r_ref, v_ref, w_ref, s_ref, pm_ref, out_ref, d_ref, q_ref, f_ref, z_ref):
    lane = lanes_of(8)
    sub = lax.broadcasted_iota(jnp.int32, (8, 128), 0)
    high = jnp.bitwise_and(lane, 4) != 0
    keep = (jnp.bitwise_and(sub, 4) != 0) == high
    for kk in range(8):
        halves = []
        for k in (2 * kk, 2 * kk + 1):
            block = r_ref[pl.ds(k * 64, 64), :].astype(F32)
            x = {}
            for i in range(8):
                tile = block[i * 8 : (i + 1) * 8]
                turned = pltpu.roll(tile, 4, 0)
                other = jnp.where(high, pltpu.roll(turned, 4, 1), pltpu.roll(turned, 124, 1))
                x[i >> 2, (i >> 1) & 1, i & 1] = jnp.where(keep, tile, other)
            for i in range(2):
                for j in range(2):
                    x[0, i, j], x[1, i, j] = swap_pair(x[0, i, j], x[1, i, j], 16, lane)
            for i in range(2):
                for j in range(2):
                    x[i, 0, j], x[i, 1, j] = swap_pair(x[i, 0, j], x[i, 1, j], 2, lane)
            for i in range(2):
                for j in range(2):
                    x[i, j, 0], x[i, j, 1] = swap_pair(x[i, j, 0], x[i, j, 1], 1, lane)
            halves.append(x)
        for a4 in range(2):
            for p in range(2):
                for a0 in range(2):
                    both = jnp.concatenate([h[a4, p, a0] for h in halves], 0).astype(BF)
                    q_ref[pl.ds((a4 * 2 + a0) * 128 + kk * 16, 16), pl.ds(p * 128, 128)] = both
    d_ref[...] = dot(v_ref[0], q_ref[...], NT)
    regroup(d_ref, q_ref, 2, 1)
    d_ref[...] = dot(v_ref[1], q_ref[...], NT)
    regroup(d_ref, q_ref, 64, 32)
    d_ref[...] = dot(v_ref[2], q_ref[...], NT)
    regroup(d_ref, q_ref, 64, 32)
    state = dot(q_ref[...], v_ref[3], NN).astype(BF)
    f_ref[...] = state
    for g in range(4):
        for p in range(2):
            z_ref[pl.ds(p * 128, 128), pl.ds(g * 128, 128)] = f_ref[pl.ds(g * 128, 128), pl.ds(p * 128, 128)]
    moved = dot(pm_ref[...], z_ref[...], NN).astype(F32)
    for b4 in range(2):
        for g in range(4):
            part = moved[b4 * 128 : (b4 + 1) * 128, g * 128 : (g + 1) * 128].reshape(16, 8, 128)
            out_ref[b4, g, :, 0] = part.astype(BF)
    rows = f_ref[...].astype(F32)
    flips = (
        jnp.concatenate([rows[256:], rows[:256]], 0),
        swap_rows(rows, 16),
        swap_rows(rows, 128),
        swap_rows(rows, 8),
    )
    image = None
    for k in range(4):
        signed = (flips[k] * jnp.concatenate([s_ref[k], s_ref[k]], 1).astype(F32)).astype(BF)
        term = dot(signed, w_ref[k], NT)
        image = term if image is None else image + term
    image = image.astype(BF)
    for g in range(4):
        for p in range(2):
            z_ref[pl.ds(p * 128, 128), pl.ds(g * 128, 128)] = image[g * 128 : (g + 1) * 128, p * 128 : (p + 1) * 128]
    moved = dot(pm_ref[...], z_ref[...], NN)
    for b4 in range(2):
        for g in range(4):
            part = moved[b4 * 128 : (b4 + 1) * 128, g * 128 : (g + 1) * 128].reshape(16, 8, 128)
            out_ref[b4, g, :, 1] = part.astype(BF)


def swap_rows(rows, half):
    n = rows.shape[0] // (2 * half)
    r = rows.reshape(n, 2, half, rows.shape[1])
    return jnp.concatenate([r[:, 1:], r[:, :1]], 1).reshape(rows.shape)


PM2 = reorder((2, 4, 2, 2, 8), (2, 4, 3, 0, 1))


def col_phase(r2, col, image, signs):
    out = pl.pallas_call(
        col_kernel,
        out_shape=jax.ShapeDtypeStruct((2, 4, 16, 2, 8, 128), BF),
        scratch_shapes=[
            pltpu.VMEM((256, 512), F32),
            pltpu.VMEM((512, 256), BF),
            pltpu.VMEM((512, 256), BF),
            pltpu.VMEM((256, 512), BF),
        ],
        name="cols",
    )(r2.reshape(1024, 128), col, image, signs, jnp.asarray(PM2, BF))
    return out.reshape(128, 16, 128)


def post_kernel(r_ref, pm_ref, f_ref, i_ref):
    for e in range(4):
        x = r_ref[pl.ds(e * 512, 512), :].astype(F32).reshape(32, 2, 8, 128)
        x = jnp.concatenate([x[:, h].reshape(256, 128) for h in range(2)], 1).astype(BF)
        moved = dot(pm_ref[...], x, NN)
        for p in range(2):
            f_ref[p, e] = moved[p * 128 : (p + 1) * 128, :128].astype(BF)
            i_ref[p, e] = moved[p * 128 : (p + 1) * 128, 128:]


PM3 = reorder((32, 2, 4), (1, 0, 2))


def post(r3):
    f, i = pl.pallas_call(
        post_kernel,
        out_shape=(jax.ShapeDtypeStruct((2, 4, 128, 128), BF), jax.ShapeDtypeStruct((2, 4, 128, 128), F32)),
        name="post",
    )(r3.reshape(2048, 128), jnp.asarray(PM3, BF))
    return f.reshape(2, 1, 1, 4, 128, 128), i.reshape(2, 1, 1, 4, 128, 128)


PT = reorder((2, 32, 4), (0, 2, 1))
C1 = reorder((2, 32, 4), (1, 0, 2))
C0 = reorder((2, 2, 2, 2, 2, 2, 4), (0, 6, 2, 1, 5, 3, 4))
R4 = reorder((2, 2, 8, 2, 4), (0, 4, 1, 3, 2))


def prep_kernel(flip_ref, mask_ref, mid_ref, g_ref, b_ref, p_ref, row_ref, col_ref, image_ref, sign_ref):
    pt = p_ref[0]

    def whole(real, imag):
        return jnp.concatenate(
            [jnp.concatenate([real, -imag], 1), jnp.concatenate([imag, real], 1)], 0
        )

    def moved(idx, left, right):
        v = whole(g_ref[idx, 0], g_ref[idx, 1])
        if left is not None:
            v = dot(left, v, NN).astype(BF)
        if right is not None:
            v = dot(v, right, NT).astype(BF)
        return v

    row_ref[0] = moved(1, pt, p_ref[1])
    row_ref[1] = moved(3, pt, pt)
    row_ref[2] = moved(5, pt, pt)
    row_ref[3] = moved(7, None, pt)
    col_ref[0] = moved(0, pt, p_ref[2])
    col_ref[1] = moved(2, pt, None)
    col_ref[2] = moved(4, p_ref[3], pt)
    col_ref[3] = dot(pt, whole(g_ref[6, 0], g_ref[6, 1]), NT).astype(BF)
    out_col = lax.broadcasted_iota(jnp.int32, (128, 128), 0)
    in_col = lax.broadcasted_iota(jnp.int32, (128, 128), 1)
    spot = lax.broadcasted_iota(jnp.int32, (512, 128), 0)
    o = jnp.bitwise_and(spot, 31)
    b = jnp.bitwise_and(o, 16) + jnp.bitwise_and(o, 7) * 2 + jnp.bitwise_and(jnp.right_shift(o, 3), 1)
    a = jnp.right_shift(spot, 8) * 16 + jnp.bitwise_and(jnp.right_shift(spot, 7), 1) + mid_ref[0]
    index = (a * 32 + b) * 128
    for k in range(4):
        onehot = (out_col == jnp.bitwise_xor(in_col, flip_ref[k])).astype(F32).astype(BF)
        sign = parity_sign(jnp.bitwise_and(out_col, mask_ref[k]))
        parts = [(dot(b_ref[k, q], onehot, NN) * sign).astype(BF) for q in range(2)]
        image_ref[k] = whole(parts[0], parts[1])
        sign_ref[k] = parity_sign(jnp.bitwise_and(index, mask_ref[k])).astype(BF)


def prep(gates, blocks, flips, masks, a_mid):
    smem = pl.BlockSpec(memory_space=pltpu.SMEM)
    vmem = pl.BlockSpec(memory_space=pltpu.VMEM)
    square = jax.ShapeDtypeStruct((4, 256, 256), BF)
    return pl.pallas_call(
        prep_kernel,
        in_specs=[smem, smem, smem, vmem, vmem, vmem],
        out_shape=(square, square, square, jax.ShapeDtypeStruct((4, 512, 128), BF)),
        name="prep",
    )(flips, masks, a_mid.reshape(1).astype(jnp.int32), gates, blocks, jnp.asarray(np.stack([PT, C1, C0, R4]), BF))


def local(amplitudes, layer_gates, pauli_blocks, flip_masks, phase_masks):
    a_mid = lax.axis_index("zl") * 4 + lax.axis_index("x1") * 2
    row, col, image, signs = prep(layer_gates, pauli_blocks, flip_masks, phase_masks, a_mid)
    r1 = exchange(pre(amplitudes), E1)
    r2 = exchange(row_phase(r1, row), E2)
    r3 = exchange(col_phase(r2, col, image, signs), E3)
    return post(r3)


def solution(mesh):
    fine = Mesh(mesh.devices.reshape(FINE_SIZES), FINE)
    spec = P(None, ("zl2", "zl", "x1", "x0"), ("zh", "y", "c"), None, None, None)
    return jax.shard_map(
        local,
        mesh=fine,
        in_specs=(spec, P(), P(), P(), P()),
        out_specs=(spec, spec),
        check_vma=False,
    )
```

profile of v0, /device:TPU:72, one launch (start us, length us, event | category | flops | bytes accessed | tf_op | source)
XLA Modules:
  0.0 130.8 jit_solution(12705604044213168512)
XLA Ops:
  0.6 3.0 %pre.1 = bf16[1024,128]{1,0:T(8,128)(2,1)} custom-call(bf16[2,4,128,128]{3,2,1,0:T(8,128)(2,1)} %bitcast.20, bf16[128,128]{1,0:T(8,128)(2,1)} %constant.27.clone.pr_ref.pc_ref, bf16[128,128]{1,0:T(8,128)(2,1)} %constant.27.clone.pr_ref.pc_ref, bf16[256,256]{1,0:T(8,128)(2,1)} %constant.28.clone.pm_ref), custom_call_target="tpu_custom_call" | custom-call | tf_op jit(solution)/shard_map/pre/pallas_call | solution.py:88
  3.6 21.4 %all-to-all-start = ((bf16[64,16,128]{2,1,0:T(8,128)(2,1)}), bf16[64,16,128]{2,1,0:T(8,128)(2,1)S(1)}, u32[]{:S(2)}, u32[]{:S(2)}) async-start(bf16[64,16,128]{2,1,0:T(8,128)(2,1)} %bitcast.18), calls=%async_computation | async-start | bytes 524288 | tf_op jit(solution)/shard_map/all_to_all | solution.py:21
  25.1 3.8 %prep.1 = (bf16[4,256,256]{2,1,0:T(8,128)(2,1)}, bf16[4,256,256]{2,1,0:T(8,128)(2,1)}, bf16[4,256,256]{2,1,0:T(8,128)(2,1)}, bf16[4,512,128]{2,1,0:T(8,128)(2,1)}) custom-call(s32[4]{0:T(128)} %flip_ref.1, s32[4]{0:T(128)} %mask_ref.1, s32[1]{0:T(128)} %bitcast.3.mid_ref, bf16[8,2,128,128]{3,2,1,0:T(8,128)(2,1)} %g_ref.1, bf16[4,2,128,128]{3,2,1,0:T(8,128)(2,1)} %b_ref.1, ...), custom_call_target="tpu_custom_call" | custom-call | tf_op jit(solution)/shard_map/prep/pallas_call | solution.py:302
  28.8 18.1 %all-to-all-done = bf16[64,16,128]{2,1,0:T(8,128)(2,1)S(1)} async-done(((bf16[64,16,128]{2,1,0:T(8,128)(2,1)}), bf16[64,16,128]{2,1,0:T(8,128)(2,1)S(1)}, u32[]{:S(2)}, u32[]{:S(2)}) %all-to-all-start) | async-done | bytes 262176 | tf_op jit(solution)/shard_map/all_to_all | solution.py:21
  46.9 0.0 copy-start
  46.9 0.7 copy-done
  47.6 3.7 %rows.1 = bf16[1024,128]{1,0:T(8,128)(2,1)} custom-call(bf16[1024,128]{1,0:T(8,128)(2,1)} %bitcast.17, bf16[4,256,256]{2,1,0:T(8,128)(2,1)} %get-tuple-element.8.v_ref), custom_call_target="tpu_custom_call" | custom-call | tf_op jit(solution)/shard_map/rows/pallas_call | solution.py:129
  51.3 26.2 %all_to_all.15 = bf16[256,4,128]{2,1,0:T(4,128)(2,1)} all-to-all(bf16[256,4,128]{2,1,0:T(4,128)(2,1)} %bitcast.19), channel_id=1, replica_groups=mesh['zl2'=2,'zl'=4,'x1'=2,'x0'=2,'zh'=2,'y'=8,'c'=2] {'zl','x1','x0','y..., dimensions={0} | all-to-all | bytes 524288 | tf_op jit(solution)/shard_map/all_to_all | solution.py:21
  77.5 5.2 %cols.1 = bf16[2,4,16,2,8,128]{5,4,3,2,1,0:T(8,128)(2,1)} custom-call(bf16[1024,128]{1,0:T(8,128)(2,1)} %bitcast.16, bf16[4,256,256]{2,1,0:T(8,128)(2,1)} %get-tuple-element.9.v_ref, bf16[4,256,256]{2,1,0:T(8,128)(2,1)} %get-tuple-element.10.w_ref, bf16[4,512,128]{2,1,0:T(8,128)(2,1)} %get-tuple-element.11.s_ref, bf16[256,256]{1,0:T(8,128)(2,1)} %constant.29.clone.pm_ref), custom_call_target="tpu_custom_call" | custom-call | tf_op jit(solution)/shard_map/cols/pallas_call | solution.py:217
  82.6 45.9 %all_to_all.16 = bf16[128,16,128]{2,1,0:T(8,128)(2,1)} all-to-all(bf16[128,16,128]{2,1,0:T(8,128)(2,1)} %bitcast.14), channel_id=1, replica_groups=mesh['zl2'=2,'zl'=4,'x1'=2,'x0'=2,'zh'=2,'y'=8,'c'=2] {'zh','zl2','x0','..., dimensions={0} | all-to-all | bytes 1048576 | tf_op jit(solution)/shard_map/all_to_all | solution.py:21
  128.6 2.2 %post.1 = (bf16[2,4,128,128]{3,2,1,0:T(8,128)(2,1)}, f32[2,4,128,128]{3,2,1,0:T(8,128)}) custom-call(bf16[2048,128]{1,0:T(8,128)(2,1)} %bitcast.15, bf16[256,256]{1,0:T(8,128)(2,1)} %constant.30.clone.pm_ref), custom_call_target="tpu_custom_call" | custom-call | tf_op jit(solution)/shard_map/post/pallas_call | solution.py:245
Async XLA Ops:
  3.6 43.3 %all-to-all-start = ((bf16[64,16,128]{2,1,0:T(8,128)(2,1)}), bf16[64,16,128]{2,1,0:T(8,128)(2,1)S(1)}, u32[]{:S(2)}, u32[]{:S(2)}) async-start(bf16[64,16,128]{2,1,0:T(8,128)(2,1)} %bitcast.18), calls=%async_computation | async-start | bytes 524288 | tf_op jit(solution)/shard_map/all_to_all | solution.py:21
  46.9 0.7 copy-start
where the time goes:
time: 131 us
  blocking collectives  72.1 us (55%)
  starting transfers between devices  21.4 us (16%)
  waiting for transfers between devices  18.1 us (14%)
  Pallas kernels  17.8 us (14%)
    all_to_all x2, blocking collectives, exchange(): return lax.all_to_all(value, axes, split_axis=0, concat_axis=0, tiled=True)  72.1 us
    all_to_all x1, starting transfers between devices, exchange(): return lax.all_to_all(value, axes, split_axis=0, concat_axis=0, tiled=True)  21.4 us
    all_to_all x1, waiting for transfers between devices, exchange(): return lax.all_to_all(value, axes, split_axis=0, concat_axis=0, tiled=True)  18.1 us
    pallas_call x1, Pallas kernels, col_phase(): pl.pallas_call(col_kernel, out_shape=jax.ShapeDtypeStruct((2, 4, 16, 2, 8...  5.16 us
    pallas_call x1, Pallas kernels, prep(): pl.pallas_call(prep_kernel, in_specs=[smem, smem, smem, vmem, vmem, vmem]...  3.77 us
    pallas_call x1, Pallas kernels, row_phase(): pl.pallas_call(row_kernel, out_shape=jax.ShapeDtypeStruct((1024, 128), BF...  3.67 us
    pallas_call x1, Pallas kernels, pre(): pl.pallas_call(pre_kernel, out_shape=jax.ShapeDtypeStruct((1024, 128), BF...  2.98 us
  transfers between devices with their start and end apart: 1, of which 1 were waited for; matrix products, arithmetic and copies ran while one was open for 0% of the time, Pallas kernels for 3%

commit v1 on v0

--- a/solution.py
+++ b/solution.py
@@ -32,6 +32,14 @@
     return (source[:, None] == np.arange(source.size)[None, :]).astype(np.float32)
 
 
+VMEM = pl.BlockSpec(memory_space=pltpu.VMEM)
+SMEM = pl.BlockSpec(memory_space=pltpu.SMEM)
+
+
+def near(value):
+    return pltpu.with_memory_space_constraint(value, pltpu.VMEM)
+
+
 def dot(a, b, dims):
     return lax.dot_general(a, b, dims, preferred_element_type=F32)
 
@@ -87,7 +95,9 @@
 def pre(amplitudes):
     out = pl.pallas_call(
         pre_kernel,
-        out_shape=jax.ShapeDtypeStruct((1024, 128), BF),
+        in_specs=[VMEM] * 4,
+        out_specs=VMEM,
+        out_shape=pltpu.VMEM((1024, 128), BF),
         scratch_shapes=[pltpu.VMEM((256, 512), BF)],
         name="pre",
     )(amplitudes.reshape(2, 4, 128, 128), jnp.asarray(PR, BF), jnp.asarray(PC, BF), jnp.asarray(PM1, BF))
@@ -128,10 +138,12 @@
 def row_phase(r1, row):
     out = pl.pallas_call(
         row_kernel,
-        out_shape=jax.ShapeDtypeStruct((1024, 128), BF),
+        in_specs=[VMEM] * 2,
+        out_specs=VMEM,
+        out_shape=pltpu.VMEM((1024, 128), BF),
         scratch_shapes=[pltpu.VMEM((256, 512), BF), pltpu.VMEM((256, 512), F32), pltpu.VMEM((512, 256), BF)],
         name="rows",
-    )(r1.reshape(1024, 128), row)
+    )(near(r1.reshape(1024, 128)), near(row))
     return out.reshape(256, 4, 128)
 
 
@@ -216,7 +228,9 @@
 def col_phase(r2, col, image, signs):
     out = pl.pallas_call(
         col_kernel,
-        out_shape=jax.ShapeDtypeStruct((2, 4, 16, 2, 8, 128), BF),
+        in_specs=[VMEM] * 5,
+        out_specs=VMEM,
+        out_shape=pltpu.VMEM((2, 4, 16, 2, 8, 128), BF),
         scratch_shapes=[
             pltpu.VMEM((256, 512), F32),
             pltpu.VMEM((512, 256), BF),
@@ -224,7 +238,7 @@
             pltpu.VMEM((256, 512), BF),
         ],
         name="cols",
-    )(r2.reshape(1024, 128), col, image, signs, jnp.asarray(PM2, BF))
+    )(near(r2.reshape(1024, 128)), near(col), near(image), near(signs), near(jnp.asarray(PM2, BF)))
     return out.reshape(128, 16, 128)
 
 
@@ -245,8 +259,9 @@
     f, i = pl.pallas_call(
         post_kernel,
         out_shape=(jax.ShapeDtypeStruct((2, 4, 128, 128), BF), jax.ShapeDtypeStruct((2, 4, 128, 128), F32)),
+        in_specs=[VMEM] * 2,
         name="post",
-    )(r3.reshape(2048, 128), jnp.asarray(PM3, BF))
+    )(near(r3.reshape(2048, 128)), near(jnp.asarray(PM3, BF)))
     return f.reshape(2, 1, 1, 4, 128, 128), i.reshape(2, 1, 1, 4, 128, 128)
 
 
@@ -296,13 +311,12 @@
 
 
 def prep(gates, blocks, flips, masks, a_mid):
-    smem = pl.BlockSpec(memory_space=pltpu.SMEM)
-    vmem = pl.BlockSpec(memory_space=pltpu.VMEM)
-    square = jax.ShapeDtypeStruct((4, 256, 256), BF)
+    square = pltpu.VMEM((4, 256, 256), BF)
     return pl.pallas_call(
         prep_kernel,
-        in_specs=[smem, smem, smem, vmem, vmem, vmem],
-        out_shape=(square, square, square, jax.ShapeDtypeStruct((4, 512, 128), BF)),
+        in_specs=[SMEM] * 3 + [VMEM] * 3,
+        out_specs=(VMEM,) * 4,
+        out_shape=(square, square, square, pltpu.VMEM((4, 512, 128), BF)),
         name="prep",
     )(flips, masks, a_mid.reshape(1).astype(jnp.int32), gates, blocks, jnp.asarray(np.stack([PT, C1, C0, R4]), BF))
 

time: 131 us -> 125 us (0.954)
  Pallas kernels: 17.8 us -> 11.9 us
    pallas_call x4, Pallas kernels: 15.6 us -> 10.7 us  [the longest x1 3.01 us: prep(): pl.pallas_call(prep_kernel, in_specs=[SMEM] * 3 + [VMEM] * 3, out_specs=(...]
  transfers between devices with their start and end apart: 1 -> 1, of which waited for: 1 -> 1; matrix products, arithmetic and copies ran while one was open for 0% -> 0% of each run, Pallas kernels for 3% -> 2%
where the time goes in v1:
time: 125 us
  blocking collectives  71.9 us (58%)
  starting transfers between devices  21.4 us (17%)
  waiting for transfers between devices  18.8 us (15%)
  Pallas kernels  11.9 us (10%)
    all_to_all x2, blocking collectives, exchange(): return lax.all_to_all(value, axes, split_axis=0, concat_axis=0, tiled=True)  71.9 us
    all_to_all x1, starting transfers between devices, exchange(): return lax.all_to_all(value, axes, split_axis=0, concat_axis=0, tiled=True)  21.4 us
    all_to_all x1, waiting for transfers between devices, exchange(): return lax.all_to_all(value, axes, split_axis=0, concat_axis=0, tiled=True)  18.8 us
    pallas_call x1, Pallas kernels, prep(): pl.pallas_call(prep_kernel, in_specs=[SMEM] * 3 + [VMEM] * 3, out_specs=(...  3.01 us
    pallas_call x1, Pallas kernels, pre(): pl.pallas_call(pre_kernel, in_specs=[VMEM] * 4, out_specs=VMEM, out_shape...  2.99 us
    pallas_call x1, Pallas kernels, col_phase(): pl.pallas_call(col_kernel, in_specs=[VMEM] * 5, out_specs=VMEM, out_shape...  2.91 us
  transfers between devices with their start and end apart: 1, of which 1 were waited for; matrix products, arithmetic and copies ran while one was open for 0% of the time, Pallas kernels for 2%

profile of v1, /device:TPU:72, one launch (start us, length us, event | category | flops | bytes accessed | tf_op | source)
XLA Modules:
  0.0 124.7 jit_solution(2031043975542249038)
XLA Ops:
  0.6 3.0 %pre.1 = bf16[1024,128]{1,0:T(8,128)(2,1)} custom-call(bf16[2,4,128,128]{3,2,1,0:T(8,128)(2,1)} %bitcast.19, bf16[128,128]{1,0:T(8,128)(2,1)} %constant.27.clone.pr_ref.pc_ref, bf16[128,128]{1,0:T(8,128)(2,1)} %constant.27.clone.pr_ref.pc_ref, bf16[256,256]{1,0:T(8,128)(2,1)} %constant.28.clone.pm_ref), custom_call_target="tpu_custom_call" | custom-call | tf_op jit(solution)/shard_map/pre/pallas_call | solution.py:96
  3.6 21.4 %all-to-all-start = ((bf16[64,16,128]{2,1,0:T(8,128)(2,1)}), bf16[64,16,128]{2,1,0:T(8,128)(2,1)S(1)}, u32[]{:S(2)}, u32[]{:S(2)}) async-start(bf16[64,16,128]{2,1,0:T(8,128)(2,1)} %bitcast.1), calls=%async_computation | async-start | bytes 524288 | tf_op jit(solution)/shard_map/all_to_all | solution.py:21
  25.1 3.0 %prep.1 = (bf16[4,256,256]{2,1,0:T(8,128)(2,1)S(1)}, bf16[4,256,256]{2,1,0:T(8,128)(2,1)S(1)}, bf16[4,256,256]{2,1,0:T(8,128)(2,1)S(1)}, bf16[4,512,128]{2,1,0:T(8,128)(2,1)S(1)}) custom-call(s32[4]{0:T(128)} %flip_ref.1, s32[4]{0:T(128)} %mask_ref.1, s32[1]{0:T(128)} %bitcast.3.mid_ref, bf16[8,2,128,128]{3,2,1,0:T(8,128)(2,1)} %g_ref.1, ...), custom_call_target="tpu_custom_call" | custom-call | tf_op jit(solution)/shard_map/prep/pallas_call | solution.py:315
  28.1 18.8 %all-to-all-done = bf16[64,16,128]{2,1,0:T(8,128)(2,1)S(1)} async-done(((bf16[64,16,128]{2,1,0:T(8,128)(2,1)}), bf16[64,16,128]{2,1,0:T(8,128)(2,1)S(1)}, u32[]{:S(2)}, u32[]{:S(2)}) %all-to-all-start) | async-done | bytes 262176 | tf_op jit(solution)/shard_map/all_to_all | solution.py:21
  46.9 1.8 %rows.1 = bf16[1024,128]{1,0:T(8,128)(2,1)S(1)} custom-call(bf16[1024,128]{1,0:T(8,128)(2,1)S(1)} %bitcast.17, bf16[4,256,256]{2,1,0:T(8,128)(2,1)S(1)} %get-tuple-element.8.v_ref), custom_call_target="tpu_custom_call" | custom-call | tf_op jit(solution)/shard_map/rows/pallas_call | solution.py:139
  48.7 0.0 copy-start.1
  48.7 26.0 %all_to_all.15 = bf16[256,4,128]{2,1,0:T(4,128)(2,1)S(1)} all-to-all(bf16[256,4,128]{2,1,0:T(4,128)(2,1)S(1)} %bitcast.18), channel_id=1, replica_groups=mesh['zl2'=2,'zl'=4,'x1'=2,'x0'=2,'zh'=2,'y'=8,'c'=2] {'zl','x1','x0','y..., dimensions={0} | all-to-all | bytes 524288 | tf_op jit(solution)/shard_map/all_to_all | solution.py:21
  74.7 0.0 copy-done.1
  74.7 2.9 %cols.1 = bf16[2,4,16,2,8,128]{5,4,3,2,1,0:T(8,128)(2,1)S(1)} custom-call(bf16[1024,128]{1,0:T(8,128)(2,1)S(1)} %bitcast.16, bf16[4,256,256]{2,1,0:T(8,128)(2,1)S(1)} %get-tuple-element.9.v_ref, bf16[4,256,256]{2,1,0:T(8,128)(2,1)S(1)} %get-tuple-element.10.w_ref, bf16[4,512,128]{2,1,0:T(8,128)(2,1)S(1)} %get-tuple-element.11.s_ref, ...), custom_call_target="tpu_custom_call" | custom-call | tf_op jit(solution)/shard_map/cols/pallas_call | solution.py:229
  77.6 0.0 copy-start
  77.6 45.9 %all_to_all.16 = bf16[128,16,128]{2,1,0:T(8,128)(2,1)S(1)} all-to-all(bf16[128,16,128]{2,1,0:T(8,128)(2,1)S(1)} %bitcast.14), channel_id=1, replica_groups=mesh['zl2'=2,'zl'=4,'x1'=2,'x0'=2,'zh'=2,'y'=8,'c'=2] {'zh','zl2','x0','..., dimensions={0} | all-to-all | bytes 1048576 | tf_op jit(solution)/shard_map/all_to_all | solution.py:21
  123.6 0.0 copy-done
  123.6 1.2 post.1
Async XLA Ops:
  3.6 43.3 %all-to-all-start = ((bf16[64,16,128]{2,1,0:T(8,128)(2,1)}), bf16[64,16,128]{2,1,0:T(8,128)(2,1)S(1)}, u32[]{:S(2)}, u32[]{:S(2)}) async-start(bf16[64,16,128]{2,1,0:T(8,128)(2,1)} %bitcast.1), calls=%async_computation | async-start | bytes 524288 | tf_op jit(solution)/shard_map/all_to_all | solution.py:21
  48.7 26.0 %copy-start.1 = (bf16[256,256]{1,0:T(8,128)(2,1)S(1)}, bf16[256,256]{1,0:T(8,128)(2,1)}, u32[]{:S(2)}) copy-start(bf16[256,256]{1,0:T(8,128)(2,1)} %constant.29.clone.pm_ref) | copy-start | bytes 393220
  77.6 45.9 %copy-start = (bf16[256,256]{1,0:T(8,128)(2,1)S(1)}, bf16[256,256]{1,0:T(8,128)(2,1)}, u32[]{:S(2)}) copy-start(bf16[256,256]{1,0:T(8,128)(2,1)} %constant.30.clone.pm_ref) | copy-start | bytes 393220

commit v2 on v1

--- a/solution.py
+++ b/solution.py
@@ -33,6 +33,7 @@
 
 
 VMEM = pl.BlockSpec(memory_space=pltpu.VMEM)
+ANY = pl.BlockSpec(memory_space=pl.ANY)
 SMEM = pl.BlockSpec(memory_space=pltpu.SMEM)
 
 
@@ -70,21 +71,42 @@
         for g in range(4):
             t = [d_ref[pl.ds(p * 128 + i * 32, 32), pl.ds(g * 128, 128)] for i in range(4)]
             for s, block in enumerate(swap_quads(t, hi, lo, lane)):
-                q_ref[pl.ds(g * 128 + s * 32, 32), pl.ds(p * 128, 128)] = block.astype(BF)
-
-
-def pre_kernel(amp_ref, pr_ref, pc_ref, pm_ref, out_ref, z_ref):
+                q_ref[pl.ds(g * 128 + s * 32, 32), pl.ds(p * 128, 128)] = block
+
+
+def pre_kernel(amp_ref, pr_ref, pc_ref, pm_ref, out_ref, in_v, pr_v, pc_v, pm_v, z_ref, out_v, in_sem, const_sem, out_sem):
+    loads = [pltpu.make_async_copy(amp_ref.at[:, e], in_v.at[:, e], in_sem.at[e]) for e in range(4)]
+    consts = [
+        pltpu.make_async_copy(src, dst, const_sem.at[i])
+        for i, (src, dst) in enumerate(((pr_ref, pr_v), (pc_ref, pc_v), (pm_ref, pm_v)))
+    ]
+    consts[0].start()
+    loads[0].start()
+    consts[1].start()
+    consts[2].start()
+    for e in range(1, 4):
+        loads[e].start()
     lane = lanes_of(32)
+    stores = []
     for e in range(4):
-        for p in range(2):
-            turned = dot(pr_ref[...], amp_ref[p, e], NN).astype(BF)
-            y = dot(pc_ref[...], turned, NT)
+        if e == 0:
+            consts[0].wait()
+            consts[1].wait()
+        loads[e].wait()
+        for p in range(2):
+            turned = dot(pr_v[...], in_v[p, e], NN).astype(BF)
+            y = dot(pc_v[...], turned, NT)
             t = [y[i * 32 : (i + 1) * 32] for i in range(4)]
             for i, block in enumerate(swap_quads(t, 64, 32, lane)):
-                z_ref[pl.ds(p * 128 + i * 32, 32), pl.ds(e * 128, 128)] = block.astype(BF)
-    moved = dot(pm_ref[...], z_ref[...], NN).astype(BF)
-    for e in range(4):
-        out_ref[pl.ds(e * 256, 256), :] = moved[:, e * 128 : (e + 1) * 128]
+                z_ref[e, pl.ds(p * 128 + i * 32, 32), :] = block.astype(BF)
+        if e == 0:
+            consts[2].wait()
+        out_v[e] = dot(pm_v[...], z_ref[e], NN).astype(BF)
+        store = pltpu.make_async_copy(out_v.at[e], out_ref.at[pl.ds(e * 256, 256)], out_sem.at[e])
+        store.start()
+        stores.append(store)
+    for store in stores:
+        store.wait()
 
 
 PR = reorder((32, 4), (1, 0))
@@ -95,10 +117,20 @@
 def pre(amplitudes):
     out = pl.pallas_call(
         pre_kernel,
-        in_specs=[VMEM] * 4,
-        out_specs=VMEM,
-        out_shape=pltpu.VMEM((1024, 128), BF),
-        scratch_shapes=[pltpu.VMEM((256, 512), BF)],
+        in_specs=[ANY] * 4,
+        out_specs=ANY,
+        out_shape=jax.ShapeDtypeStruct((1024, 128), BF),
+        scratch_shapes=[
+            pltpu.VMEM((2, 4, 128, 128), BF),
+            pltpu.VMEM((128, 128), BF),
+            pltpu.VMEM((128, 128), BF),
+            pltpu.VMEM((256, 256), BF),
+            pltpu.VMEM((4, 256, 128), BF),
+            pltpu.VMEM((4, 256, 128), BF),
+            pltpu.SemaphoreType.DMA((4,)),
+            pltpu.SemaphoreType.DMA((3,)),
+            pltpu.SemaphoreType.DMA((4,)),
+        ],
         name="pre",
     )(amplitudes.reshape(2, 4, 128, 128), jnp.asarray(PR, BF), jnp.asarray(PC, BF), jnp.asarray(PM1, BF))
     return out.reshape(64, 16, 128)
@@ -109,13 +141,13 @@
         x = r_ref[pl.ds(b4 * 512, 512), :].astype(F32).reshape(32, 2, 8, 128)
         for c1 in range(2):
             x_ref[:, pl.ds((b4 * 2 + c1) * 128, 128)] = x[:, c1].reshape(256, 128).astype(BF)
-    d_ref[...] = dot(v_ref[0], x_ref[...], NN)
-    regroup(d_ref, q_ref, 64, 32)
-    d_ref[...] = dot(v_ref[1], q_ref[...], NT)
-    regroup(d_ref, q_ref, 64, 32)
-    d_ref[...] = dot(v_ref[2], q_ref[...], NT)
-    regroup(d_ref, q_ref, 64, 32)
-    d_ref[...] = dot(v_ref[3], q_ref[...], NT)
+    d_ref[...] = dot(v_ref[0], x_ref[...], NN).astype(BF)
+    regroup(d_ref, q_ref, 64, 32)
+    d_ref[...] = dot(v_ref[1], q_ref[...], NT).astype(BF)
+    regroup(d_ref, q_ref, 64, 32)
+    d_ref[...] = dot(v_ref[2], q_ref[...], NT).astype(BF)
+    regroup(d_ref, q_ref, 64, 32)
+    d_ref[...] = dot(v_ref[3], q_ref[...], NT).astype(BF)
     lane = lanes_of(32)
     for piece in range(4):
         x = {}
@@ -132,7 +164,7 @@
             for c1 in range(2):
                 x[b, c1, 0], x[b, c1, 1] = swap_pair(x[b, c1, 0], x[b, c1, 1], 2, lane)
         for (i, j, k), block in x.items():
-            out_ref[pl.ds((i * 4 + j * 2 + k) * 128 + piece * 32, 32), :] = block.astype(BF)
+            out_ref[pl.ds((i * 4 + j * 2 + k) * 128 + piece * 32, 32), :] = block
 
 
 def row_phase(r1, row):
@@ -141,7 +173,7 @@
         in_specs=[VMEM] * 2,
         out_specs=VMEM,
         out_shape=pltpu.VMEM((1024, 128), BF),
-        scratch_shapes=[pltpu.VMEM((256, 512), BF), pltpu.VMEM((256, 512), F32), pltpu.VMEM((512, 256), BF)],
+        scratch_shapes=[pltpu.VMEM((256, 512), BF), pltpu.VMEM((256, 512), BF), pltpu.VMEM((512, 256), BF)],
         name="rows",
     )(near(r1.reshape(1024, 128)), near(row))
     return out.reshape(256, 4, 128)
@@ -177,11 +209,11 @@
                 for a0 in range(2):
                     both = jnp.concatenate([h[a4, p, a0] for h in halves], 0).astype(BF)
                     q_ref[pl.ds((a4 * 2 + a0) * 128 + kk * 16, 16), pl.ds(p * 128, 128)] = both
-    d_ref[...] = dot(v_ref[0], q_ref[...], NT)
+    d_ref[...] = dot(v_ref[0], q_ref[...], NT).astype(BF)
     regroup(d_ref, q_ref, 2, 1)
-    d_ref[...] = dot(v_ref[1], q_ref[...], NT)
-    regroup(d_ref, q_ref, 64, 32)
-    d_ref[...] = dot(v_ref[2], q_ref[...], NT)
+    d_ref[...] = dot(v_ref[1], q_ref[...], NT).astype(BF)
+    regroup(d_ref, q_ref, 64, 32)
+    d_ref[...] = dot(v_ref[2], q_ref[...], NT).astype(BF)
     regroup(d_ref, q_ref, 64, 32)
     state = dot(q_ref[...], v_ref[3], NN).astype(BF)
     f_ref[...] = state
@@ -232,7 +264,7 @@
         out_specs=VMEM,
         out_shape=pltpu.VMEM((2, 4, 16, 2, 8, 128), BF),
         scratch_shapes=[
-            pltpu.VMEM((256, 512), F32),
+            pltpu.VMEM((256, 512), BF),
             pltpu.VMEM((512, 256), BF),
             pltpu.VMEM((512, 256), BF),
             pltpu.VMEM((256, 512), BF),

time: 125 us -> 127 us (1.016)
  Pallas kernels: 11.9 us -> 13.4 us
    pallas_call x1, Pallas kernels: 2.99 us -> 4.32 us  [pre(): pl.pallas_call(pre_kernel, in_specs=[ANY] * 4, out_specs=ANY, out_shape=j...]
where the time goes in v2:
time: 127 us; the launch traced here: 126 us
  blocking collectives  71.9 us (57%)
  starting transfers between devices  21.4 us (17%)
  waiting for transfers between devices  18.8 us (15%)
  Pallas kernels  13.4 us (11%)
    all_to_all x2, blocking collectives, exchange(): return lax.all_to_all(value, axes, split_axis=0, concat_axis=0, tiled=True)  71.9 us
    all_to_all x1, starting transfers between devices, exchange(): return lax.all_to_all(value, axes, split_axis=0, concat_axis=0, tiled=True)  21.4 us
    all_to_all x1, waiting for transfers between devices, exchange(): return lax.all_to_all(value, axes, split_axis=0, concat_axis=0, tiled=True)  18.8 us
    pallas_call x1, Pallas kernels, pre(): pl.pallas_call(pre_kernel, in_specs=[ANY] * 4, out_specs=ANY, out_shape=j...  4.32 us
    pallas_call x1, Pallas kernels, prep(): pl.pallas_call(prep_kernel, in_specs=[SMEM] * 3 + [VMEM] * 3, out_specs=(...  3.01 us
    pallas_call x1, Pallas kernels, col_phase(): pl.pallas_call(col_kernel, in_specs=[VMEM] * 5, out_specs=VMEM, out_shape...  2.95 us
  transfers between devices with their start and end apart: 1, of which 1 were waited for; matrix products, arithmetic and copies ran while one was open for 0% of the time, Pallas kernels for 2%

profile of v2, /device:TPU:72, one launch (start us, length us, event | category | flops | bytes accessed | tf_op | source)
XLA Modules:
  0.0 126.2 jit_solution(9652510153908528613)
XLA Ops:
  0.6 4.3 %pre.1 = bf16[1024,128]{1,0:T(8,128)(2,1)} custom-call(bf16[2,4,128,128]{3,2,1,0:T(8,128)(2,1)} %bitcast.20, bf16[128,128]{1,0:T(8,128)(2,1)} %constant.27.clone.pr_ref.pc_ref, bf16[128,128]{1,0:T(8,128)(2,1)} %constant.27.clone.pr_ref.pc_ref, bf16[256,256]{1,0:T(8,128)(2,1)} %constant.28.clone.pm_ref), custom_call_target="tpu_custom_call" | custom-call | tf_op jit(solution)/shard_map/pre/pallas_call | solution.py:118
  5.0 21.4 %all-to-all-start = ((bf16[64,16,128]{2,1,0:T(8,128)(2,1)}), bf16[64,16,128]{2,1,0:T(8,128)(2,1)S(1)}, u32[]{:S(2)}, u32[]{:S(2)}) async-start(bf16[64,16,128]{2,1,0:T(8,128)(2,1)} %bitcast.19), calls=%async_computation | async-start | bytes 524288 | tf_op jit(solution)/shard_map/all_to_all | solution.py:21
  26.4 3.0 %prep.1 = (bf16[4,256,256]{2,1,0:T(8,128)(2,1)S(1)}, bf16[4,256,256]{2,1,0:T(8,128)(2,1)S(1)}, bf16[4,256,256]{2,1,0:T(8,128)(2,1)S(1)}, bf16[4,512,128]{2,1,0:T(8,128)(2,1)S(1)}) custom-call(s32[4]{0:T(128)} %flip_ref.1, s32[4]{0:T(128)} %mask_ref.1, s32[1]{0:T(128)} %bitcast.3.mid_ref, bf16[8,2,128,128]{3,2,1,0:T(8,128)(2,1)} %g_ref.1, ...), custom_call_target="tpu_custom_call" | custom-call | tf_op jit(solution)/shard_map/prep/pallas_call | solution.py:347
  29.4 18.8 %all-to-all-done = bf16[64,16,128]{2,1,0:T(8,128)(2,1)S(1)} async-done(((bf16[64,16,128]{2,1,0:T(8,128)(2,1)}), bf16[64,16,128]{2,1,0:T(8,128)(2,1)S(1)}, u32[]{:S(2)}, u32[]{:S(2)}) %all-to-all-start) | async-done | bytes 262176 | tf_op jit(solution)/shard_map/all_to_all | solution.py:21
  48.3 1.9 %rows.1 = bf16[1024,128]{1,0:T(8,128)(2,1)S(1)} custom-call(bf16[1024,128]{1,0:T(8,128)(2,1)S(1)} %bitcast.17, bf16[4,256,256]{2,1,0:T(8,128)(2,1)S(1)} %get-tuple-element.8.v_ref), custom_call_target="tpu_custom_call" | custom-call | tf_op jit(solution)/shard_map/rows/pallas_call | solution.py:171
  50.2 0.0 copy-start.1
  50.2 26.0 %all_to_all.15 = bf16[256,4,128]{2,1,0:T(4,128)(2,1)S(1)} all-to-all(bf16[256,4,128]{2,1,0:T(4,128)(2,1)S(1)} %bitcast.18), channel_id=1, replica_groups=mesh['zl2'=2,'zl'=4,'x1'=2,'x0'=2,'zh'=2,'y'=8,'c'=2] {'zl','x1','x0','y..., dimensions={0} | all-to-all | bytes 524288 | tf_op jit(solution)/shard_map/all_to_all | solution.py:21
  76.2 0.0 copy-done.1
  76.2 2.9 %cols.1 = bf16[2,4,16,2,8,128]{5,4,3,2,1,0:T(8,128)(2,1)S(1)} custom-call(bf16[1024,128]{1,0:T(8,128)(2,1)S(1)} %bitcast.16, bf16[4,256,256]{2,1,0:T(8,128)(2,1)S(1)} %get-tuple-element.9.v_ref, bf16[4,256,256]{2,1,0:T(8,128)(2,1)S(1)} %get-tuple-element.10.w_ref, bf16[4,512,128]{2,1,0:T(8,128)(2,1)S(1)} %get-tuple-element.11.s_ref, ...), custom_call_target="tpu_custom_call" | custom-call | tf_op jit(solution)/shard_map/cols/pallas_call | solution.py:261
  79.1 0.0 copy-start
  79.1 45.9 %all_to_all.16 = bf16[128,16,128]{2,1,0:T(8,128)(2,1)S(1)} all-to-all(bf16[128,16,128]{2,1,0:T(8,128)(2,1)S(1)} %bitcast.14), channel_id=1, replica_groups=mesh['zl2'=2,'zl'=4,'x1'=2,'x0'=2,'zh'=2,'y'=8,'c'=2] {'zh','zl2','x0','..., dimensions={0} | all-to-all | bytes 1048576 | tf_op jit(solution)/shard_map/all_to_all | solution.py:21
  125.0 0.0 copy-done
  125.0 1.2 post.1
Async XLA Ops:
  5.0 43.3 %all-to-all-start = ((bf16[64,16,128]{2,1,0:T(8,128)(2,1)}), bf16[64,16,128]{2,1,0:T(8,128)(2,1)S(1)}, u32[]{:S(2)}, u32[]{:S(2)}) async-start(bf16[64,16,128]{2,1,0:T(8,128)(2,1)} %bitcast.19), calls=%async_computation | async-start | bytes 524288 | tf_op jit(solution)/shard_map/all_to_all | solution.py:21
  50.2 26.0 %copy-start.1 = (bf16[256,256]{1,0:T(8,128)(2,1)S(1)}, bf16[256,256]{1,0:T(8,128)(2,1)}, u32[]{:S(2)}) copy-start(bf16[256,256]{1,0:T(8,128)(2,1)} %constant.29.clone.pm_ref) | copy-start | bytes 393220
  79.1 45.9 %copy-start = (bf16[256,256]{1,0:T(8,128)(2,1)S(1)}, bf16[256,256]{1,0:T(8,128)(2,1)}, u32[]{:S(2)}) copy-start(bf16[256,256]{1,0:T(8,128)(2,1)} %constant.30.clone.pm_ref) | copy-start | bytes 393220

commit v3 on v1

--- a/solution.py
+++ b/solution.py
@@ -9,7 +9,7 @@
 FINE = ("zl2", "zl", "x1", "x0", "zh", "y", "c")
 FINE_SIZES = (2, 4, 2, 2, 2, 8, 2)
 E1 = ("zh", "zl2", "zl", "x1", "x0")
-E2 = ("zl", "x1", "x0", "y", "c")
+E2 = ("c", "zl", "x1", "x0", "y")
 E3 = ("zh", "zl2", "x0", "y", "c")
 BF = jnp.bfloat16
 F32 = jnp.float32
@@ -132,7 +132,8 @@
             for c1 in range(2):
                 x[b, c1, 0], x[b, c1, 1] = swap_pair(x[b, c1, 0], x[b, c1, 1], 2, lane)
         for (i, j, k), block in x.items():
-            out_ref[pl.ds((i * 4 + j * 2 + k) * 128 + piece * 32, 32), :] = block.astype(BF)
+            spot = (piece >> 1) * 512 + (i * 4 + j * 2 + k) * 64 + (piece & 1) * 32
+            out_ref[pl.ds(spot, 32), :] = block.astype(BF)
 
 
 def row_phase(r1, row):
@@ -155,10 +156,10 @@
     for kk in range(8):
         halves = []
         for k in (2 * kk, 2 * kk + 1):
-            block = r_ref[pl.ds(k * 64, 64), :].astype(F32)
+            blocks = [r_ref[pl.ds(c * 512 + k * 32, 32), :].astype(F32) for c in range(2)]
             x = {}
             for i in range(8):
-                tile = block[i * 8 : (i + 1) * 8]
+                tile = blocks[i & 1][(i >> 1) * 8 : (i >> 1) * 8 + 8]
                 turned = pltpu.roll(tile, 4, 0)
                 other = jnp.where(high, pltpu.roll(turned, 4, 1), pltpu.roll(turned, 124, 1))
                 x[i >> 2, (i >> 1) & 1, i & 1] = jnp.where(keep, tile, other)
@@ -267,7 +268,8 @@
 
 PT = reorder((2, 32, 4), (0, 2, 1))
 C1 = reorder((2, 32, 4), (1, 0, 2))
-C0 = reorder((2, 2, 2, 2, 2, 2, 4), (0, 6, 2, 1, 5, 3, 4))
+C0 = reorder((2, 2, 2, 2, 2, 2, 4), (0, 6, 2, 1, 4, 3, 5))
+R7 = reorder((2, 16, 2, 4), (0, 2, 1, 3))
 R4 = reorder((2, 2, 8, 2, 4), (0, 4, 1, 3, 2))
 
 
@@ -290,7 +292,7 @@
     row_ref[0] = moved(1, pt, p_ref[1])
     row_ref[1] = moved(3, pt, pt)
     row_ref[2] = moved(5, pt, pt)
-    row_ref[3] = moved(7, None, pt)
+    row_ref[3] = moved(7, p_ref[4], pt)
     col_ref[0] = moved(0, pt, p_ref[2])
     col_ref[1] = moved(2, pt, None)
     col_ref[2] = moved(4, p_ref[3], pt)
@@ -318,7 +320,7 @@
         out_specs=(VMEM,) * 4,
         out_shape=(square, square, square, pltpu.VMEM((4, 512, 128), BF)),
         name="prep",
-    )(flips, masks, a_mid.reshape(1).astype(jnp.int32), gates, blocks, jnp.asarray(np.stack([PT, C1, C0, R4]), BF))
+    )(flips, masks, a_mid.reshape(1).astype(jnp.int32), gates, blocks, jnp.asarray(np.stack([PT, C1, C0, R4, R7]), BF))
 
 
 def local(amplitudes, layer_gates, pauli_blocks, flip_masks, phase_masks):

time: 125 us -> 125 us (level)
  no operation moved by 1% of the time
where the time goes in v3:
time: 125 us
  blocking collectives  72 us (58%)
  starting transfers between devices  21.4 us (17%)
  waiting for transfers between devices  18.8 us (15%)
  Pallas kernels  11.9 us (10%)
    all_to_all x2, blocking collectives, exchange(): return lax.all_to_all(value, axes, split_axis=0, concat_axis=0, tiled=True)  72 us
    all_to_all x1, starting transfers between devices, exchange(): return lax.all_to_all(value, axes, split_axis=0, concat_axis=0, tiled=True)  21.4 us
    all_to_all x1, waiting for transfers between devices, exchange(): return lax.all_to_all(value, axes, split_axis=0, concat_axis=0, tiled=True)  18.8 us
    pallas_call x1, Pallas kernels, prep(): pl.pallas_call(prep_kernel, in_specs=[SMEM] * 3 + [VMEM] * 3, out_specs=(...  3.01 us
    pallas_call x1, Pallas kernels, pre(): pl.pallas_call(pre_kernel, in_specs=[VMEM] * 4, out_specs=VMEM, out_shape...  2.99 us
    pallas_call x1, Pallas kernels, col_phase(): pl.pallas_call(col_kernel, in_specs=[VMEM] * 5, out_specs=VMEM, out_shape...  2.91 us
  transfers between devices with their start and end apart: 1, of which 1 were waited for; matrix products, arithmetic and copies ran while one was open for 0% of the time, Pallas kernels for 2%

profile of v3, /device:TPU:72, one launch (start us, length us, event | category | flops | bytes accessed | tf_op | source)
XLA Modules:
  0.0 124.8 jit_solution(4758560203961726730)
XLA Ops:
  0.6 3.0 %pre.1 = bf16[1024,128]{1,0:T(8,128)(2,1)} custom-call(bf16[2,4,128,128]{3,2,1,0:T(8,128)(2,1)} %bitcast.19, bf16[128,128]{1,0:T(8,128)(2,1)} %constant.27.clone.pr_ref.pc_ref, bf16[128,128]{1,0:T(8,128)(2,1)} %constant.27.clone.pr_ref.pc_ref, bf16[256,256]{1,0:T(8,128)(2,1)} %constant.28.clone.pm_ref), custom_call_target="tpu_custom_call" | custom-call | tf_op jit(solution)/shard_map/pre/pallas_call | solution.py:96
  3.6 21.4 %all-to-all-start = ((bf16[64,16,128]{2,1,0:T(8,128)(2,1)}), bf16[64,16,128]{2,1,0:T(8,128)(2,1)S(1)}, u32[]{:S(2)}, u32[]{:S(2)}) async-start(bf16[64,16,128]{2,1,0:T(8,128)(2,1)} %bitcast.1), calls=%async_computation | async-start | bytes 524288 | tf_op jit(solution)/shard_map/all_to_all | solution.py:21
  25.1 3.0 %prep.1 = (bf16[4,256,256]{2,1,0:T(8,128)(2,1)S(1)}, bf16[4,256,256]{2,1,0:T(8,128)(2,1)S(1)}, bf16[4,256,256]{2,1,0:T(8,128)(2,1)S(1)}, bf16[4,512,128]{2,1,0:T(8,128)(2,1)S(1)}) custom-call(s32[4]{0:T(128)} %flip_ref.1, s32[4]{0:T(128)} %mask_ref.1, s32[1]{0:T(128)} %bitcast.3.mid_ref, bf16[8,2,128,128]{3,2,1,0:T(8,128)(2,1)} %g_ref.1, ...), custom_call_target="tpu_custom_call" | custom-call | tf_op jit(solution)/shard_map/prep/pallas_call | solution.py:317
  28.1 18.8 %all-to-all-done = bf16[64,16,128]{2,1,0:T(8,128)(2,1)S(1)} async-done(((bf16[64,16,128]{2,1,0:T(8,128)(2,1)}), bf16[64,16,128]{2,1,0:T(8,128)(2,1)S(1)}, u32[]{:S(2)}, u32[]{:S(2)}) %all-to-all-start) | async-done | bytes 262176 | tf_op jit(solution)/shard_map/all_to_all | solution.py:21
  46.9 1.8 %rows.1 = bf16[1024,128]{1,0:T(8,128)(2,1)S(1)} custom-call(bf16[1024,128]{1,0:T(8,128)(2,1)S(1)} %bitcast.17, bf16[4,256,256]{2,1,0:T(8,128)(2,1)S(1)} %get-tuple-element.8.v_ref), custom_call_target="tpu_custom_call" | custom-call | tf_op jit(solution)/shard_map/rows/pallas_call | solution.py:140
  48.7 0.0 copy-start.1
  48.7 26.3 %all_to_all.15 = bf16[256,4,128]{2,1,0:T(4,128)(2,1)S(1)} all-to-all(bf16[256,4,128]{2,1,0:T(4,128)(2,1)S(1)} %bitcast.18), channel_id=1, replica_groups=mesh['zl2'=2,'zl'=4,'x1'=2,'x0'=2,'zh'=2,'y'=8,'c'=2] {'c','zl','x1','x0..., dimensions={0} | all-to-all | bytes 524288 | tf_op jit(solution)/shard_map/all_to_all | solution.py:21
  75.1 0.0 copy-done.1
  75.1 2.9 %cols.1 = bf16[2,4,16,2,8,128]{5,4,3,2,1,0:T(8,128)(2,1)S(1)} custom-call(bf16[1024,128]{1,0:T(8,128)(2,1)S(1)} %bitcast.16, bf16[4,256,256]{2,1,0:T(8,128)(2,1)S(1)} %get-tuple-element.9.v_ref, bf16[4,256,256]{2,1,0:T(8,128)(2,1)S(1)} %get-tuple-element.10.w_ref, bf16[4,512,128]{2,1,0:T(8,128)(2,1)S(1)} %get-tuple-element.11.s_ref, ...), custom_call_target="tpu_custom_call" | custom-call | tf_op jit(solution)/shard_map/cols/pallas_call | solution.py:230
  78.0 0.0 copy-start
  78.0 45.7 %all_to_all.16 = bf16[128,16,128]{2,1,0:T(8,128)(2,1)S(1)} all-to-all(bf16[128,16,128]{2,1,0:T(8,128)(2,1)S(1)} %bitcast.14), channel_id=1, replica_groups=mesh['zl2'=2,'zl'=4,'x1'=2,'x0'=2,'zh'=2,'y'=8,'c'=2] {'zh','zl2','x0','..., dimensions={0} | all-to-all | bytes 1048576 | tf_op jit(solution)/shard_map/all_to_all | solution.py:21
  123.7 0.0 copy-done
  123.7 1.2 post.1
Async XLA Ops:
  3.6 43.3 %all-to-all-start = ((bf16[64,16,128]{2,1,0:T(8,128)(2,1)}), bf16[64,16,128]{2,1,0:T(8,128)(2,1)S(1)}, u32[]{:S(2)}, u32[]{:S(2)}) async-start(bf16[64,16,128]{2,1,0:T(8,128)(2,1)} %bitcast.1), calls=%async_computation | async-start | bytes 524288 | tf_op jit(solution)/shard_map/all_to_all | solution.py:21
  48.7 26.3 %copy-start.1 = (bf16[256,256]{1,0:T(8,128)(2,1)S(1)}, bf16[256,256]{1,0:T(8,128)(2,1)}, u32[]{:S(2)}) copy-start(bf16[256,256]{1,0:T(8,128)(2,1)} %constant.29.clone.pm_ref) | copy-start | bytes 393220
  78.0 45.7 %copy-start = (bf16[256,256]{1,0:T(8,128)(2,1)S(1)}, bf16[256,256]{1,0:T(8,128)(2,1)}, u32[]{:S(2)}) copy-start(bf16[256,256]{1,0:T(8,128)(2,1)} %constant.30.clone.pm_ref) | copy-start | bytes 393220

commit v4 on v3

--- a/solution.py
+++ b/solution.py
@@ -33,6 +33,7 @@
 
 
 VMEM = pl.BlockSpec(memory_space=pltpu.VMEM)
+ANY = pl.BlockSpec(memory_space=pl.ANY)
 SMEM = pl.BlockSpec(memory_space=pltpu.SMEM)
 
 
@@ -73,7 +74,21 @@
                 q_ref[pl.ds(g * 128 + s * 32, 32), pl.ds(p * 128, 128)] = block.astype(BF)
 
 
-def pre_kernel(amp_ref, pr_ref, pc_ref, pm_ref, out_ref, z_ref):
+def picks(size, source_of):
+    row = lax.broadcasted_iota(jnp.int32, (size, 128), 0)
+    col = lax.broadcasted_iota(jnp.int32, (size, 128), 1)
+    source = source_of(row)
+    parts = [(source == col + off).astype(F32) for off in range(0, size, 128)]
+    return (jnp.concatenate(parts, 1) if len(parts) > 1 else parts[0]).astype(BF)
+
+
+def pre_kernel(amp_hbm, out_ref, amp_ref, pr_ref, pc_ref, pm_ref, z_ref, sem):
+    load = pltpu.make_async_copy(amp_hbm, amp_ref, sem)
+    load.start()
+    pr_ref[...] = picks(128, lambda r: (r & 31) * 4 + (r >> 5))
+    pc_ref[...] = picks(128, lambda r: ((r >> 1) & 15) * 8 + (r & 1) * 4 + (r >> 5))
+    pm_ref[...] = picks(256, lambda r: ((r >> 2) & 1) * 128 + (r & 3) * 32 + (r >> 4) * 2 + ((r >> 3) & 1))
+    load.wait()
     lane = lanes_of(32)
     for e in range(4):
         for p in range(2):
@@ -87,20 +102,22 @@
         out_ref[pl.ds(e * 256, 256), :] = moved[:, e * 128 : (e + 1) * 128]
 
 
-PR = reorder((32, 4), (1, 0))
-PC = reorder((16, 2, 4), (2, 0, 1))
-PM1 = reorder((2, 4, 16, 2), (2, 3, 0, 1))
-
-
 def pre(amplitudes):
     out = pl.pallas_call(
         pre_kernel,
-        in_specs=[VMEM] * 4,
+        in_specs=[ANY],
         out_specs=VMEM,
         out_shape=pltpu.VMEM((1024, 128), BF),
-        scratch_shapes=[pltpu.VMEM((256, 512), BF)],
+        scratch_shapes=[
+            pltpu.VMEM((2, 4, 128, 128), BF),
+            pltpu.VMEM((128, 128), BF),
+            pltpu.VMEM((128, 128), BF),
+            pltpu.VMEM((256, 256), BF),
+            pltpu.VMEM((256, 512), BF),
+            pltpu.SemaphoreType.DMA,
+        ],
         name="pre",
-    )(amplitudes.reshape(2, 4, 128, 128), jnp.asarray(PR, BF), jnp.asarray(PC, BF), jnp.asarray(PM1, BF))
+    )(amplitudes.reshape(2, 4, 128, 128))
     return out.reshape(64, 16, 128)
 
 
@@ -148,7 +165,7 @@
     return out.reshape(256, 4, 128)
 
 
-def col_kernel(r_ref, v_ref, w_ref, s_ref, pm_ref, out_ref, d_ref, q_ref, f_ref, z_ref):
+def col_kernel(r_ref, v_ref, w_ref, s_ref, pm_ref, out_ref, d_ref, q_ref, f_ref, z_ref, g_ref):
     lane = lanes_of(8)
     sub = lax.broadcasted_iota(jnp.int32, (8, 128), 0)
     high = jnp.bitwise_and(lane, 4) != 0
@@ -194,18 +211,20 @@
         for g in range(4):
             part = moved[b4 * 128 : (b4 + 1) * 128, g * 128 : (g + 1) * 128].reshape(16, 8, 128)
             out_ref[b4, g, :, 0] = part.astype(BF)
-    rows = f_ref[...].astype(F32)
-    flips = (
-        jnp.concatenate([rows[256:], rows[:256]], 0),
-        swap_rows(rows, 16),
-        swap_rows(rows, 128),
-        swap_rows(rows, 8),
-    )
-    image = None
     for k in range(4):
-        signed = (flips[k] * jnp.concatenate([s_ref[k], s_ref[k]], 1).astype(F32)).astype(BF)
-        term = dot(signed, w_ref[k], NT)
-        image = term if image is None else image + term
+        for r in range(0, 512, 32):
+            source = r ^ (256, 0, 128, 0)[k]
+            for p in range(2):
+                half = pl.ds(p * 128, 128)
+                if k == 1:
+                    block = jnp.concatenate([f_ref[pl.ds(r + 16, 16), half], f_ref[pl.ds(r, 16), half]], 0)
+                elif k == 3:
+                    wide = f_ref[pl.ds(r, 32), half].astype(F32)
+                    block = jnp.concatenate([wide[8:16], wide[:8], wide[24:], wide[16:24]], 0).astype(BF)
+                else:
+                    block = f_ref[pl.ds(source, 32), half]
+                g_ref[pl.ds(r, 32), pl.ds(k * 256 + p * 128, 128)] = block * s_ref[k, pl.ds(r, 32), :]
+    image = dot(g_ref[...], w_ref[...], NT)
     image = image.astype(BF)
     for g in range(4):
         for p in range(2):
@@ -215,12 +234,6 @@
         for g in range(4):
             part = moved[b4 * 128 : (b4 + 1) * 128, g * 128 : (g + 1) * 128].reshape(16, 8, 128)
             out_ref[b4, g, :, 1] = part.astype(BF)
-
-
-def swap_rows(rows, half):
-    n = rows.shape[0] // (2 * half)
-    r = rows.reshape(n, 2, half, rows.shape[1])
-    return jnp.concatenate([r[:, 1:], r[:, :1]], 1).reshape(rows.shape)
 
 
 PM2 = reorder((2, 4, 2, 2, 8), (2, 4, 3, 0, 1))
@@ -237,6 +250,7 @@
             pltpu.VMEM((512, 256), BF),
             pltpu.VMEM((512, 256), BF),
             pltpu.VMEM((256, 512), BF),
+            pltpu.VMEM((512, 1024), BF),
         ],
         name="cols",
     )(near(r2.reshape(1024, 128)), near(col), near(image), near(signs), near(jnp.asarray(PM2, BF)))
@@ -308,7 +322,7 @@
         onehot = (out_col == jnp.bitwise_xor(in_col, flip_ref[k])).astype(F32).astype(BF)
         sign = parity_sign(jnp.bitwise_and(out_col, mask_ref[k]))
         parts = [(dot(b_ref[k, q], onehot, NN) * sign).astype(BF) for q in range(2)]
-        image_ref[k] = whole(parts[0], parts[1])
+        image_ref[:, pl.ds(k * 256, 256)] = whole(parts[0], parts[1])
         sign_ref[k] = parity_sign(jnp.bitwise_and(index, mask_ref[k])).astype(BF)
 
 
@@ -318,7 +332,7 @@
         prep_kernel,
         in_specs=[SMEM] * 3 + [VMEM] * 3,
         out_specs=(VMEM,) * 4,
-        out_shape=(square, square, square, pltpu.VMEM((4, 512, 128), BF)),
+        out_shape=(square, square, pltpu.VMEM((256, 1024), BF), pltpu.VMEM((4, 512, 128), BF)),
         name="prep",
     )(flips, masks, a_mid.reshape(1).astype(jnp.int32), gates, blocks, jnp.asarray(np.stack([PT, C1, C0, R4, R7]), BF))
 

time: 125 us -> 125 us (level)
  no operation moved by 1% of the time
where the time goes in v4:
time: 125 us
  blocking collectives  72 us (58%)
  starting transfers between devices  21.4 us (17%)
  waiting for transfers between devices  18.8 us (15%)
  Pallas kernels  11.9 us (10%)
    all_to_all x2, blocking collectives, exchange(): return lax.all_to_all(value, axes, split_axis=0, concat_axis=0, tiled=True)  72 us
    all_to_all x1, starting transfers between devices, exchange(): return lax.all_to_all(value, axes, split_axis=0, concat_axis=0, tiled=True)  21.4 us
    all_to_all x1, waiting for transfers between devices, exchange(): return lax.all_to_all(value, axes, split_axis=0, concat_axis=0, tiled=True)  18.8 us
    pallas_call x1, Pallas kernels, prep(): pl.pallas_call(prep_kernel, in_specs=[SMEM] * 3 + [VMEM] * 3, out_specs=(...  3.01 us
    pallas_call x1, Pallas kernels, col_phase(): pl.pallas_call(col_kernel, in_specs=[VMEM] * 5, out_specs=VMEM, out_shape...  3 us
    pallas_call x1, Pallas kernels, pre(): pl.pallas_call(pre_kernel, in_specs=[ANY], out_specs=VMEM, out_shape=pltp...  2.92 us
  transfers between devices with their start and end apart: 1, of which 1 were waited for; matrix products, arithmetic and copies ran while one was open for 0% of the time, Pallas kernels for 2%

profile of v4, /device:TPU:72, one launch (start us, length us, event | category | flops | bytes accessed | tf_op | source)
XLA Modules:
  0.0 124.9 jit_solution(6297627991979365656)
XLA Ops:
  0.6 2.9 %pre.1 = bf16[1024,128]{1,0:T(8,128)(2,1)} custom-call(bf16[2,4,128,128]{3,2,1,0:T(8,128)(2,1)} %bitcast.19), custom_call_target="tpu_custom_call" | custom-call | tf_op jit(solution)/shard_map/pre/pallas_call | solution.py:106
  3.6 21.4 %all-to-all-start = ((bf16[64,16,128]{2,1,0:T(8,128)(2,1)}), bf16[64,16,128]{2,1,0:T(8,128)(2,1)S(1)}, u32[]{:S(2)}, u32[]{:S(2)}) async-start(bf16[64,16,128]{2,1,0:T(8,128)(2,1)} %bitcast.1), calls=%async_computation | async-start | bytes 524288 | tf_op jit(solution)/shard_map/all_to_all | solution.py:21
  25.0 3.0 %prep.1 = (bf16[4,256,256]{2,1,0:T(8,128)(2,1)S(1)}, bf16[4,256,256]{2,1,0:T(8,128)(2,1)S(1)}, bf16[256,1024]{1,0:T(8,128)(2,1)S(1)}, bf16[4,512,128]{2,1,0:T(8,128)(2,1)S(1)}) custom-call(s32[4]{0:T(128)} %flip_ref.1, s32[4]{0:T(128)} %mask_ref.1, s32[1]{0:T(128)} %bitcast.3.mid_ref, bf16[8,2,128,128]{3,2,1,0:T(8,128)(2,1)} %g_ref.1, ...), custom_call_target="tpu_custom_call" | custom-call | tf_op jit(solution)/shard_map/prep/pallas_call | solution.py:331
  28.0 18.8 %all-to-all-done = bf16[64,16,128]{2,1,0:T(8,128)(2,1)S(1)} async-done(((bf16[64,16,128]{2,1,0:T(8,128)(2,1)}), bf16[64,16,128]{2,1,0:T(8,128)(2,1)S(1)}, u32[]{:S(2)}, u32[]{:S(2)}) %all-to-all-start) | async-done | bytes 262176 | tf_op jit(solution)/shard_map/all_to_all | solution.py:21
  46.9 1.8 %rows.1 = bf16[1024,128]{1,0:T(8,128)(2,1)S(1)} custom-call(bf16[1024,128]{1,0:T(8,128)(2,1)S(1)} %bitcast.17, bf16[4,256,256]{2,1,0:T(8,128)(2,1)S(1)} %get-tuple-element.8.v_ref), custom_call_target="tpu_custom_call" | custom-call | tf_op jit(solution)/shard_map/rows/pallas_call | solution.py:157
  48.7 0.0 copy-start.1
  48.7 26.3 %all_to_all.15 = bf16[256,4,128]{2,1,0:T(4,128)(2,1)S(1)} all-to-all(bf16[256,4,128]{2,1,0:T(4,128)(2,1)S(1)} %bitcast.18), channel_id=1, replica_groups=mesh['zl2'=2,'zl'=4,'x1'=2,'x0'=2,'zh'=2,'y'=8,'c'=2] {'c','zl','x1','x0..., dimensions={0} | all-to-all | bytes 524288 | tf_op jit(solution)/shard_map/all_to_all | solution.py:21
  75.0 0.0 copy-done.1
  75.0 3.0 %cols.1 = bf16[2,4,16,2,8,128]{5,4,3,2,1,0:T(8,128)(2,1)S(1)} custom-call(bf16[1024,128]{1,0:T(8,128)(2,1)S(1)} %bitcast.16, bf16[4,256,256]{2,1,0:T(8,128)(2,1)S(1)} %get-tuple-element.9.v_ref, bf16[256,1024]{1,0:T(8,128)(2,1)S(1)} %get-tuple-element.10.w_ref, bf16[4,512,128]{2,1,0:T(8,128)(2,1)S(1)} %get-tuple-element.11.s_ref, bf16[256,256]{1,0:T(8,128)(2,1)S(1)} %copy-done.1), custom_call_target="tpu_custom_call" | custom-call | tf_op jit(solution)/shard_map/cols/pallas_call | solution.py:243
  78.0 0.0 copy-start
  78.0 45.7 %all_to_all.16 = bf16[128,16,128]{2,1,0:T(8,128)(2,1)S(1)} all-to-all(bf16[128,16,128]{2,1,0:T(8,128)(2,1)S(1)} %bitcast.14), channel_id=1, replica_groups=mesh['zl2'=2,'zl'=4,'x1'=2,'x0'=2,'zh'=2,'y'=8,'c'=2] {'zh','zl2','x0','..., dimensions={0} | all-to-all | bytes 1048576 | tf_op jit(solution)/shard_map/all_to_all | solution.py:21
  123.7 0.0 copy-done
  123.7 1.2 post.1
Async XLA Ops:
  3.6 43.3 %all-to-all-start = ((bf16[64,16,128]{2,1,0:T(8,128)(2,1)}), bf16[64,16,128]{2,1,0:T(8,128)(2,1)S(1)}, u32[]{:S(2)}, u32[]{:S(2)}) async-start(bf16[64,16,128]{2,1,0:T(8,128)(2,1)} %bitcast.1), calls=%async_computation | async-start | bytes 524288 | tf_op jit(solution)/shard_map/all_to_all | solution.py:21
  48.7 26.3 %copy-start.1 = (bf16[256,256]{1,0:T(8,128)(2,1)S(1)}, bf16[256,256]{1,0:T(8,128)(2,1)}, u32[]{:S(2)}) copy-start(bf16[256,256]{1,0:T(8,128)(2,1)} %constant.23.clone.pm_ref) | copy-start | bytes 393220
  78.0 45.7 %copy-start = (bf16[256,256]{1,0:T(8,128)(2,1)S(1)}, bf16[256,256]{1,0:T(8,128)(2,1)}, u32[]{:S(2)}) copy-start(bf16[256,256]{1,0:T(8,128)(2,1)} %constant.24.clone.pm_ref) | copy-start | bytes 393220

commit v5 on v3

--- a/solution.py
+++ b/solution.py
@@ -10,7 +10,7 @@
 FINE_SIZES = (2, 4, 2, 2, 2, 8, 2)
 E1 = ("zh", "zl2", "zl", "x1", "x0")
 E2 = ("c", "zl", "x1", "x0", "y")
-E3 = ("zh", "zl2", "x0", "y", "c")
+E3 = ("c", "x0", "zh", "zl2", "y")
 BF = jnp.bfloat16
 F32 = jnp.float32
 NT = (((1,), (1,)), ((), ()))
@@ -190,10 +190,10 @@
         for p in range(2):
             z_ref[pl.ds(p * 128, 128), pl.ds(g * 128, 128)] = f_ref[pl.ds(g * 128, 128), pl.ds(p * 128, 128)]
     moved = dot(pm_ref[...], z_ref[...], NN).astype(F32)
-    for b4 in range(2):
+    for b in range(4):
         for g in range(4):
-            part = moved[b4 * 128 : (b4 + 1) * 128, g * 128 : (g + 1) * 128].reshape(16, 8, 128)
-            out_ref[b4, g, :, 0] = part.astype(BF)
+            part = moved[b * 64 : (b + 1) * 64, g * 128 : (g + 1) * 128].reshape(8, 8, 128)
+            out_ref[b & 1, g & 1, b >> 1, g >> 1, :, 0] = part.astype(BF)
     rows = f_ref[...].astype(F32)
     flips = (
         jnp.concatenate([rows[256:], rows[:256]], 0),
@@ -211,10 +211,10 @@
         for p in range(2):
             z_ref[pl.ds(p * 128, 128), pl.ds(g * 128, 128)] = image[g * 128 : (g + 1) * 128, p * 128 : (p + 1) * 128]
     moved = dot(pm_ref[...], z_ref[...], NN)
-    for b4 in range(2):
+    for b in range(4):
         for g in range(4):
-            part = moved[b4 * 128 : (b4 + 1) * 128, g * 128 : (g + 1) * 128].reshape(16, 8, 128)
-            out_ref[b4, g, :, 1] = part.astype(BF)
+            part = moved[b * 64 : (b + 1) * 64, g * 128 : (g + 1) * 128].reshape(8, 8, 128)
+            out_ref[b & 1, g & 1, b >> 1, g >> 1, :, 1] = part.astype(BF)
 
 
 def swap_rows(rows, half):
@@ -223,7 +223,7 @@
     return jnp.concatenate([r[:, 1:], r[:, :1]], 1).reshape(rows.shape)
 
 
-PM2 = reorder((2, 4, 2, 2, 8), (2, 4, 3, 0, 1))
+PM2 = reorder((2, 4, 2, 2, 8), (2, 3, 4, 0, 1))
 
 
 def col_phase(r2, col, image, signs):
@@ -231,7 +231,7 @@
         col_kernel,
         in_specs=[VMEM] * 5,
         out_specs=VMEM,
-        out_shape=pltpu.VMEM((2, 4, 16, 2, 8, 128), BF),
+        out_shape=pltpu.VMEM((2, 2, 2, 2, 8, 2, 8, 128), BF),
         scratch_shapes=[
             pltpu.VMEM((256, 512), F32),
             pltpu.VMEM((512, 256), BF),
@@ -245,7 +245,8 @@
 
 def post_kernel(r_ref, pm_ref, f_ref, i_ref):
     for e in range(4):
-        x = r_ref[pl.ds(e * 512, 512), :].astype(F32).reshape(32, 2, 8, 128)
+        x = jnp.concatenate([r_ref[pl.ds(i * 512 + e * 128, 128), :] for i in range(4)], 0)
+        x = x.astype(F32).reshape(32, 2, 8, 128)
         x = jnp.concatenate([x[:, h].reshape(256, 128) for h in range(2)], 1).astype(BF)
         moved = dot(pm_ref[...], x, NN)
         for p in range(2):
@@ -253,7 +254,7 @@
             i_ref[p, e] = moved[p * 128 : (p + 1) * 128, 128:]
 
 
-PM3 = reorder((32, 2, 4), (1, 0, 2))
+PM3 = reorder((2, 2, 8, 2, 4), (3, 1, 2, 0, 4))
 
 
 def post(r3):

time: 125 us -> 123 us (0.984)
  the two profiles are of different devices: /device:TPU:72 before, /device:TPU:67 now
where the time goes in v5:
time: 123 us
  blocking collectives  73.6 us (60%)
  starting transfers between devices  20.8 us (17%)
  waiting for transfers between devices  16 us (13%)
  Pallas kernels  11.9 us (10%)
    all_to_all x2, blocking collectives, exchange(): return lax.all_to_all(value, axes, split_axis=0, concat_axis=0, tiled=True)  73.6 us
    all_to_all x1, starting transfers between devices, exchange(): return lax.all_to_all(value, axes, split_axis=0, concat_axis=0, tiled=True)  20.8 us
    all_to_all x1, waiting for transfers between devices, exchange(): return lax.all_to_all(value, axes, split_axis=0, concat_axis=0, tiled=True)  16 us
    pallas_call x1, Pallas kernels, prep(): pl.pallas_call(prep_kernel, in_specs=[SMEM] * 3 + [VMEM] * 3, out_specs=(...  3.01 us
    pallas_call x1, Pallas kernels, pre(): pl.pallas_call(pre_kernel, in_specs=[VMEM] * 4, out_specs=VMEM, out_shape...  2.99 us
    pallas_call x1, Pallas kernels, col_phase(): pl.pallas_call(col_kernel, in_specs=[VMEM] * 5, out_specs=VMEM, out_shape...  2.91 us
  transfers between devices with their start and end apart: 1, of which 1 were waited for; matrix products, arithmetic and copies ran while one was open for 0% of the time, Pallas kernels for 2%

profile of v5, /device:TPU:67, one launch (start us, length us, event | category | flops | bytes accessed | tf_op | source)
XLA Modules:
  0.0 123.1 jit_solution(4264187674262028650)
XLA Ops:
  0.6 3.0 %pre.1 = bf16[1024,128]{1,0:T(8,128)(2,1)} custom-call(bf16[2,4,128,128]{3,2,1,0:T(8,128)(2,1)} %bitcast.19, bf16[128,128]{1,0:T(8,128)(2,1)} %constant.25.clone.pr_ref.pc_ref, bf16[128,128]{1,0:T(8,128)(2,1)} %constant.25.clone.pr_ref.pc_ref, bf16[256,256]{1,0:T(8,128)(2,1)} %constant.26.clone.pm_ref), custom_call_target="tpu_custom_call" | custom-call | tf_op jit(solution)/shard_map/pre/pallas_call | solution.py:96
  3.6 20.8 %all-to-all-start = ((bf16[64,16,128]{2,1,0:T(8,128)(2,1)}), bf16[64,16,128]{2,1,0:T(8,128)(2,1)S(1)}, u32[]{:S(2)}, u32[]{:S(2)}) async-start(bf16[64,16,128]{2,1,0:T(8,128)(2,1)} %bitcast.1), calls=%async_computation | async-start | bytes 524288 | tf_op jit(solution)/shard_map/all_to_all | solution.py:21
  24.5 3.0 %prep.1 = (bf16[4,256,256]{2,1,0:T(8,128)(2,1)S(1)}, bf16[4,256,256]{2,1,0:T(8,128)(2,1)S(1)}, bf16[4,256,256]{2,1,0:T(8,128)(2,1)S(1)}, bf16[4,512,128]{2,1,0:T(8,128)(2,1)S(1)}) custom-call(s32[4]{0:T(128)} %flip_ref.1, s32[4]{0:T(128)} %mask_ref.1, s32[1]{0:T(128)} %bitcast.3.mid_ref, bf16[8,2,128,128]{3,2,1,0:T(8,128)(2,1)} %g_ref.1, ...), custom_call_target="tpu_custom_call" | custom-call | tf_op jit(solution)/shard_map/prep/pallas_call | solution.py:318
  27.5 16.0 %all-to-all-done = bf16[64,16,128]{2,1,0:T(8,128)(2,1)S(1)} async-done(((bf16[64,16,128]{2,1,0:T(8,128)(2,1)}), bf16[64,16,128]{2,1,0:T(8,128)(2,1)S(1)}, u32[]{:S(2)}, u32[]{:S(2)}) %all-to-all-start) | async-done | bytes 262176 | tf_op jit(solution)/shard_map/all_to_all | solution.py:21
  43.5 1.8 %rows.1 = bf16[1024,128]{1,0:T(8,128)(2,1)S(1)} custom-call(bf16[1024,128]{1,0:T(8,128)(2,1)S(1)} %bitcast.17, bf16[4,256,256]{2,1,0:T(8,128)(2,1)S(1)} %get-tuple-element.8.v_ref), custom_call_target="tpu_custom_call" | custom-call | tf_op jit(solution)/shard_map/rows/pallas_call | solution.py:140
  45.4 0.0 copy-start
  45.4 29.7 %all_to_all.15 = bf16[256,4,128]{2,1,0:T(4,128)(2,1)S(1)} all-to-all(bf16[256,4,128]{2,1,0:T(4,128)(2,1)S(1)} %bitcast.18), channel_id=1, replica_groups=mesh['zl2'=2,'zl'=4,'x1'=2,'x0'=2,'zh'=2,'y'=8,'c'=2] {'c','zl','x1','x0..., dimensions={0} | all-to-all | bytes 524288 | tf_op jit(solution)/shard_map/all_to_all | solution.py:21
  75.0 0.0 copy-done
  75.0 2.9 %cols.1 = bf16[2,2,2,2,8,2,8,128]{7,6,5,4,3,2,1,0:T(8,128)(2,1)S(1)} custom-call(bf16[1024,128]{1,0:T(8,128)(2,1)S(1)} %bitcast.16, bf16[4,256,256]{2,1,0:T(8,128)(2,1)S(1)} %get-tuple-element.9.v_ref, bf16[4,256,256]{2,1,0:T(8,128)(2,1)S(1)} %get-tuple-element.10.w_ref, bf16[4,512,128]{2,1,0:T(8,128)(2,1)S(1)} %get-tuple-element.11.s_ref, ...), custom_call_target="tpu_custom_call" | custom-call | tf_op jit(solution)/shard_map/cols/pallas_call | solution.py:230
  78.0 0.0 copy-start.1
  78.0 43.9 %all_to_all.16 = bf16[128,16,128]{2,1,0:T(8,128)(2,1)S(1)} all-to-all(bf16[128,16,128]{2,1,0:T(8,128)(2,1)S(1)} %bitcast.14), channel_id=1, replica_groups=mesh['zl2'=2,'zl'=4,'x1'=2,'x0'=2,'zh'=2,'y'=8,'c'=2] {'c','x0','zh','zl..., dimensions={0} | all-to-all | bytes 1048576 | tf_op jit(solution)/shard_map/all_to_all | solution.py:21
  121.9 0.0 copy-done.1
  121.9 1.2 post.1
Async XLA Ops:
  3.6 39.9 %all-to-all-start = ((bf16[64,16,128]{2,1,0:T(8,128)(2,1)}), bf16[64,16,128]{2,1,0:T(8,128)(2,1)S(1)}, u32[]{:S(2)}, u32[]{:S(2)}) async-start(bf16[64,16,128]{2,1,0:T(8,128)(2,1)} %bitcast.1), calls=%async_computation | async-start | bytes 524288 | tf_op jit(solution)/shard_map/all_to_all | solution.py:21
  45.4 29.7 %copy-start = (bf16[256,256]{1,0:T(8,128)(2,1)S(1)}, bf16[256,256]{1,0:T(8,128)(2,1)}, u32[]{:S(2)}) copy-start(bf16[256,256]{1,0:T(8,128)(2,1)} %constant.26.clone.pm_ref) | copy-start | bytes 393220
  78.0 44.0 %copy-start.1 = (bf16[256,256]{1,0:T(8,128)(2,1)S(1)}, bf16[256,256]{1,0:T(8,128)(2,1)}, u32[]{:S(2)}) copy-start(bf16[256,256]{1,0:T(8,128)(2,1)} %constant.27.clone.pm_ref) | copy-start | bytes 393220
